TPU v7x, 256 devices: a whole 4x4x8 slice. The times are simulated.
256 devices in a mesh: blk: 256 (over y, z, x, core).
Axes of the slice: x: 4, y: 4, z: 8, core: 2. Of those that a mesh axis runs over, the one named last changes fastest.
Arguments:
- state: float32 [768, 6, 16, 256], P('blk'), may hold values from -0.5 to 3, as said below
- wall_dist: float32 [768, 16, 256], P('blk'), may hold values from 0.2 to 2
- block_metric: float32 [768, 10], P('blk'), may hold values from -1 to 1
- inflow: float32 [6], replicated, may hold values from 0.5 to 1
- counts: int32 [256], P('blk'), may hold values from 1 to 3, as said below
- links: int32 [768, 6, 4], P('blk'), may hold values from 0 to 767, as said below
Outputs:
- tendency: float32 [768, 6, 16, 256], P('blk')
- time_step: float32 [], replicated
Inputs may be any that keep to these rules, and one draw needn't show every extreme that they name: `state`: field 0 lies in 0.8 to 1.2, fields 1 to 3 in -0.5 to 0.5, field 4 in 2 to 3, field 5 in 0 to 0.4. `counts`: every device has 1 to 3 blocks in use, in its first slots; some device has 3. `links`: code 3 marks an interface, 0 far field, 1 wall, 2 outflow. Interfaces join blocks in use and are mutual: if face f of b names face h of g with orientation o, then face h of g names face f of b with the inverse reindexing. i faces pair with i faces (any o of 0 to 7); j and k faces pair with j or k faces, with o even. A partner block lies on a device whose index differs by at most 2 along the axis, counted cyclically. Of the faces of one device, at most 1 i face and at most 3 j or k faces name blocks on any one other device, and some device has 3 j or k faces naming blocks of one other device. For boundary faces and unused slots the partner is the block itself.
All inputs are finite; a program needn't handle non-finite values.
Results may differ from a plain program's by a relative error of at most 0.0003.
Values sent between devices are 32-bit elements; how exact they have to be, the bound alone decides.
No kernel may reach another device: no remote copies, remote signals or barrier semaphores. Data moves between devices by JAX's collectives and lax.ppermute only.
A program may use at most 128 MiB of HBM per device.

v0:
```python
import jax
import jax.numpy as jnp
from jax import lax
from jax.experimental import pallas as pl
from jax.experimental.pallas import tpu as pltpu
from jax.sharding import PartitionSpec as P

NI = 16
NJ = 16
NK = 16
SLOTS = 3
FIELDS = 6
LANES = 128
OFFSETS = (-2, -1, 1, 2)

GAMMA = 1.4
PROD_COEF = 0.1355
DEST_COEF = 3.239
COURANT = 0.5
WALL_SIGNS = (1.0, -1.0, -1.0, -1.0, 1.0, -1.0)

SEND = (8, 8, LANES)
PLAN = 128
PLAN_I = 16
PLAN_FACE = 32

f32 = jnp.float32
i32 = jnp.int32


def iota(shape, axis):
    return lax.broadcasted_iota(i32, shape, axis)


def pick(values, index, axis):
    return jnp.take_along_axis(values, index, axis=axis, mode="promise_in_bounds")


def geometry(metric_ref, slot):
    normals = [
        [(1.0 if d == e else 0.0) + 0.25 * metric_ref[slot, 3 * d + e] for e in range(3)] for d in range(3)
    ]
    return normals, 1.0 + 0.25 * metric_ref[slot, 9]


def area_of(normal):
    total = normal[0] * normal[0] + normal[1] * normal[1] + normal[2] * normal[2]
    return jnp.sqrt(total)


def splat(value, shape):
    return jnp.full(shape, value, f32)


def primitives(cons):
    inverse = 1.0 / cons[0]
    velocity = [cons[1 + c] * inverse for c in range(3)]
    kinetic = cons[1] * velocity[0] + cons[2] * velocity[1] + cons[3] * velocity[2]
    pressure = (GAMMA - 1.0) * (cons[4] - 0.5 * kinetic)
    sound = jnp.sqrt(GAMMA * pressure * inverse)
    return inverse, velocity, pressure, sound


def fluxes_of(cons, prim, normal, area):
    _, velocity, pressure, sound = prim
    normal_vel = normal[0] * velocity[0] + normal[1] * velocity[1] + normal[2] * velocity[2]
    fluxes = [
        cons[0] * normal_vel,
        cons[1] * normal_vel + pressure * normal[0],
        cons[2] * normal_vel + pressure * normal[1],
        cons[3] * normal_vel + pressure * normal[2],
        (cons[4] + pressure) * normal_vel,
        cons[5] * normal_vel,
    ]
    return fluxes, jnp.abs(normal_vel) + sound * area


def edge(own, ghost, normal, area, sign):
    own_prim = primitives(own)
    ghost_prim = primitives(ghost)
    own_flux, own_speed = fluxes_of(own, own_prim, normal, area)
    ghost_flux, ghost_speed = fluxes_of(ghost, ghost_prim, normal, area)
    speed = sign * jnp.maximum(own_speed, ghost_speed)
    flux = [own_flux[f] + ghost_flux[f] - speed * (ghost[f] - own[f]) for f in range(FIELDS)]
    return flux, ghost_prim[1]


def split(values):
    return values[:, :LANES], values[:, LANES:]


def shifted_up(values, axis_dir):
    low, high = split(values)
    if axis_dir == 0:
        low, high = pltpu.roll(low, NI - 1, 0), pltpu.roll(high, NI - 1, 0)
    elif axis_dir == 1:
        low, high = pltpu.roll(low, LANES - NK, 1), pltpu.roll(high, LANES - NK, 1)
        low = jnp.where(iota(low.shape, 1) < LANES - NK, low, high)
    else:
        low, high = pltpu.roll(low, LANES - 1, 1), pltpu.roll(high, LANES - 1, 1)
    return jnp.concatenate([low, high], axis=1)


def shifted_down(values, axis_dir):
    low, high = split(values)
    if axis_dir == 0:
        low, high = pltpu.roll(low, 1, 0), pltpu.roll(high, 1, 0)
    elif axis_dir == 1:
        low, high = pltpu.roll(low, NK, 1), pltpu.roll(high, NK, 1)
        high = jnp.where(iota(high.shape, 1) < NK, low, high)
    else:
        low, high = pltpu.roll(low, 1, 1), pltpu.roll(high, 1, 1)
    return jnp.concatenate([low, high], axis=1)


def placed(compact, axis_dir):
    if axis_dir == 1:
        low = jnp.concatenate([compact, pltpu.roll(compact, 64, 1)], axis=0)
        high = jnp.concatenate([pltpu.roll(compact, 96, 1), pltpu.roll(compact, 32, 1)], axis=0)
        return low, high
    lane = iota((8, LANES), 1)
    index = lane // NK + jnp.where(lane % NK == NK - 1, 48, 32)
    rows = []
    for a in range(2):
        rows.append(jnp.concatenate([pick(compact, index + (64 * a + 8 * b), 1) for b in range(2)], axis=1))
    both = jnp.concatenate(rows, axis=0)
    return both, both


def put_high(values, high, axis_dir):
    if axis_dir == 0:
        return jnp.where(iota(values.shape, 0) == NI - 1, high, values)
    if axis_dir == 1:
        first, second = split(values)
        second = jnp.where(iota(second.shape, 1) >= LANES - NK, high, second)
        return jnp.concatenate([first, second], axis=1)
    return jnp.where(iota(values.shape, 1) % NK == NK - 1, high, values)


def put_low(values, low, axis_dir):
    if axis_dir == 0:
        return jnp.where(iota(values.shape, 0) == 0, low, values)
    if axis_dir == 1:
        first, second = split(values)
        first = jnp.where(iota(first.shape, 1) < NK, low, first)
        return jnp.concatenate([first, second], axis=1)
    return jnp.where(iota(values.shape, 1) % NK == 0, low, values)


def write_edges(values, slot, table_jk, table_i):
    lane = iota((8, LANES), 1)
    t = lane % NK
    group = lane // NK % 4
    index = jnp.where(
        group == 0,
        t,
        jnp.where(group == 1, LANES - NK + t, NK * (t % 8) + jnp.where(group == 3, NK - 1, 0)),
    )
    second = (group == 1) | ((group >= 2) & (t >= 8))
    for f in range(FIELDS):
        halves = []
        for a in range(2):
            rows = values[f][8 * a : 8 * a + 8]
            halves.append(jnp.where(second, pick(rows[:, LANES:], index, 1), pick(rows[:, :LANES], index, 1)))
        table_jk[slot, f] = jnp.where(lane < 64, halves[0], halves[1])
        for face in range(2):
            row = values[f][(NI - 1) * face : (NI - 1) * face + 1]
            at = 8 * (2 * slot + face) + f
            table_i[0, at : at + 1, :] = row[:, :LANES]
            table_i[1, at : at + 1, :] = row[:, LANES:]


def make_plan(links_ref, device, dev_count, plan_ref, mask_ref):
    def entry(slot, face):
        code, block, other = links_ref[slot, 0, face], links_ref[slot, 1, face], links_ref[slot, 2, face]
        partner_dev = lax.div(block, SLOTS)
        away = lax.rem(partner_dev - device + dev_count, dev_count)
        space = jnp.where(
            away == dev_count - 2, 0, jnp.where(away == dev_count - 1, 1, jnp.where(away == 1, 2, jnp.where(away == 2, 3, 4)))
        )
        space = jnp.where(code == 3, space, 4)
        return space, block - SLOTS * partner_dev, other

    for n in range(PLAN_I + 5):
        plan_ref[n] = 0
    for n in range(5):
        mask_ref[n] = 0
        mask_ref[8 + n] = 0
    entries = {}
    for slot in range(SLOTS):
        for face in range(6):
            space, partner_slot, other = entry(slot, face)
            if face < 2:
                plan_ref[PLAN_I + space] = 2 * slot + face
                plan_ref[PLAN_FACE + 2 * (6 * slot + face)] = jnp.where(
                    space < 4, 2 * SLOTS + space, 2 * partner_slot + (other & 1)
                )
                continue
            count = mask_ref[8 + space]
            mask_ref[8 + space] = count + 1
            plan_ref[3 * space + jnp.where(space < 4, jnp.minimum(count, 2), 0)] = 4 * slot + face - 2
            key = 4 * partner_slot + ((other - 2) & 3)
            mask_ref[space] = mask_ref[space] | lax.shift_left(jnp.int32(1), key)
            entries[slot, face] = (space, partner_slot, key)
    for (slot, face), (space, partner_slot, key) in entries.items():
        below = mask_ref[space] & (lax.shift_left(jnp.int32(1), key) - 1)
        below = below - (lax.shift_right_logical(below, 1) & 0x555)
        below = (below & 0x333) + (lax.shift_right_logical(below, 2) & 0x333)
        below = (below + lax.shift_right_logical(below, 4)) & 0xF0F
        rank = jnp.minimum((below + lax.shift_right_logical(below, 8)) & 0xF, 2)
        at = PLAN_FACE + 2 * (6 * slot + face)
        plan_ref[at] = jnp.where(space < 4, SLOTS + space, partner_slot)
        plan_ref[at + 1] = NK * jnp.where(space < 4, rank, key & 3)


def write_sends(table_jk, table_i, plan_ref, send_refs):
    lane = iota((8, LANES), 1)
    group = lane // NK % 4
    base = (lane & 64) | (lane % NK)
    row = iota((8, LANES), 0)
    for n in range(len(OFFSETS)):
        chosen = []
        for q in range(3):
            source = plan_ref[3 * n + q]
            index = base + NK * (source & 3)
            slot = lax.shift_right_logical(source, 2)
            chosen.append([pick(table_jk[slot, f], index, 1) for f in range(FIELDS)])
        for f in range(FIELDS):
            send_refs[n][f] = jnp.where(group == 0, chosen[0][f], jnp.where(group == 1, chosen[1][f], chosen[2][f]))
        at = pl.multiple_of(8 * plan_ref[PLAN_I + n], 8)
        first = table_i[0, pl.ds(at, 8), :]
        second = table_i[1, pl.ds(at, 8), :]
        send_refs[n][6] = jnp.where(row < FIELDS, first, 0.0)
        send_refs[n][7] = jnp.where(row < FIELDS, second, 0.0)


def jk_ghosts(slot, table_jk, links_ref, plan_ref, far):
    lane = iota((8, LANES), 1)
    row = iota((8, LANES), 0)
    t = lane % NK
    group = lane // NK % 4
    gathered = None
    code = jnp.zeros((8, LANES), i32)
    row_index = row
    for face in range(2, 6):
        at = PLAN_FACE + 2 * (6 * slot + face)
        source, start = plan_ref[at], plan_ref[at + 1]
        orient = links_ref[slot, 3, face]
        first_rev = lax.shift_right_logical(orient, 1) & 1
        second_rev = lax.shift_right_logical(orient, 2) & 1
        index = ((lane & 64) ^ (64 * first_rev)) + (t ^ (15 * second_rev)) + start
        here = group == face - 2
        code = jnp.where(here, links_ref[slot, 0, face], code)
        row_index = jnp.where(here, row ^ (7 * first_rev), row_index)
        layers = [pick(table_jk[source, f], index, 1) for f in range(FIELDS)]
        gathered = layers if gathered is None else [jnp.where(here, new, old) for new, old in zip(layers, gathered)]
    own = [table_jk[slot, f] for f in range(FIELDS)]
    ghosts = []
    joined, distant, wall = code == 3, code == 0, code == 1
    for f in range(FIELDS):
        mirrored = own[f] if WALL_SIGNS[f] > 0 else jnp.where(wall, -own[f], own[f])
        ghosts.append(jnp.where(joined, pick(gathered[f], row_index, 0), jnp.where(distant, far[f], mirrored)))
    return own, ghosts


def i_ghosts(table_i, ghost_i, links_ref, plan_ref, far):
    row = iota((8, 2 * LANES), 0)
    flat = iota((8, 2 * LANES), 1)
    code = jnp.zeros((8, 2 * LANES), i32)
    orient = jnp.zeros((8, 2 * LANES), i32)
    for n in range(2 * SLOTS):
        slot, face = n // 2, n % 2
        at = pl.multiple_of(8 * plan_ref[PLAN_FACE + 2 * (6 * slot + face)], 8)
        for b in range(2):
            ghost_i[b, 8 * n : 8 * n + 8, :] = table_i[b, pl.ds(at, 8), :]
        code = jnp.where(row == n, links_ref[slot, 0, face], code)
        orient = jnp.where(row == n, links_ref[slot, 3, face], orient)
    first = (flat // NK) ^ (15 * ((orient >> 1) & 1))
    second = (flat % NK) ^ (15 * ((orient >> 2) & 1))
    source = jnp.where((orient & 1) == 1, NK * second + first, NK * first + second)
    upper = source >= LANES
    index = source & (LANES - 1)
    joined, distant, wall = code == 3, code == 0, code == 1
    own, ghosts = [], []
    for f in range(FIELDS):
        mine = jnp.concatenate([table_i[b, pl.ds(f, 8, stride=8), :] for b in range(2)], axis=1)
        halves = [ghost_i[b, pl.ds(f, 8, stride=8), :] for b in range(2)]
        layer = []
        for b in range(2):
            at = slice(b * LANES, (b + 1) * LANES)
            layer.append(jnp.where(upper[:, at], pick(halves[1], index[:, at], 1), pick(halves[0], index[:, at], 1)))
        layer = jnp.concatenate(layer, axis=1)
        mirrored = mine if WALL_SIGNS[f] > 0 else jnp.where(wall, -mine, mine)
        own.append(mine)
        ghosts.append(jnp.where(joined, layer, jnp.where(distant, far[f], mirrored)))
    return own, ghosts


def far_field(inflow_ref):
    density, pressure = inflow_ref[0], inflow_ref[4]
    velocity = [inflow_ref[1 + c] for c in range(3)]
    squares = velocity[0] * velocity[0] + velocity[1] * velocity[1] + velocity[2] * velocity[2]
    energy = pressure * (1.0 / (GAMMA - 1.0)) + 0.5 * density * squares
    return [density] + [density * v for v in velocity] + [energy, density * inflow_ref[5]]


def section(load, distance_ref, links_ref, counts_ref, metric_ref, inflow_ref, plan_ref, table_jk, table_i, ghost_i, edge_i, store):
    far = far_field(inflow_ref)
    own, ghosts = i_ghosts(table_i, ghost_i, links_ref, plan_ref, far)
    row = iota((8, 2 * LANES), 0)
    normal = [None] * 3
    for e in range(3):
        value = splat((1.0 if e == 0 else 0.0) + 0.25 * metric_ref[0, e], row.shape)
        for slot in range(1, SLOTS):
            value = jnp.where(row // 2 == slot, (1.0 if e == 0 else 0.0) + 0.25 * metric_ref[slot, e], value)
        normal[e] = value
    sign = jnp.where(row % 2 == 1, 1.0, -1.0)
    flux, velocity = edge(own, ghosts, normal, area_of(normal), sign)
    for n, value in enumerate(flux + velocity):
        edge_i[n] = value

    group = iota((8, LANES), 1) // NK % 4
    sign_jk = jnp.where(group % 2 == 1, 1.0, -1.0)

    def one(slot):
        normals, volume = geometry(metric_ref, slot)
        own, ghosts = jk_ghosts(slot, table_jk, links_ref, plan_ref, far)
        lane_normal = [jnp.where(group < 2, normals[1][e], normals[2][e]) for e in range(3)]
        edge_flux, edge_velocity = edge(own, ghosts, lane_normal, area_of(lane_normal), sign_jk)
        cons = load(slot)
        prim = primitives(cons)
        inverse, velocity = prim[0], prim[1]
        half_inverse = splat(0.5, (1, 1)) / splat(volume, (1, 1))
        net = [None] * FIELDS
        differences = []
        for d in range(3):
            area = area_of([splat(normals[d][e], (1, 1)) for e in range(3)])
            fluxes, speed = fluxes_of(cons, prim, normals[d], area)
            speed = jnp.maximum(speed, shifted_up(speed, d))
            for f in range(FIELDS):
                if d == 0:
                    low = edge_i[f, 2 * slot : 2 * slot + 1, :]
                    high = edge_i[f, 2 * slot + 1 : 2 * slot + 2, :]
                else:
                    low, high = placed(edge_flux[f], d)
                above = fluxes[f] + shifted_up(fluxes[f], d) - speed * (shifted_up(cons[f], d) - cons[f])
                above = put_high(above, high, d)
                change = above - put_low(shifted_down(above, d), low, d)
                net[f] = change if net[f] is None else net[f] + change
            change = []
            for c in range(3):
                if d == 0:
                    low = edge_i[FIELDS + c, 2 * slot : 2 * slot + 1, :]
                    high = edge_i[FIELDS + c, 2 * slot + 1 : 2 * slot + 2, :]
                else:
                    low, high = placed(edge_velocity[c], d)
                change.append(put_high(shifted_up(velocity[c], d), high, d) - put_low(shifted_down(velocity[c], d), low, d))
            differences.append(change)
        squares = None
        for e in range(3):
            scaled = [splat(normals[d][e], (1, 1)) * half_inverse for d in range(3)]
            for c in range(3):
                entry = scaled[0] * differences[0][c] + scaled[1] * differences[1][c] + scaled[2] * differences[2][c]
                squares = entry * entry if squares is None else squares + entry * entry
        ratio = cons[5] * inverse / distance_ref[slot]
        source = PROD_COEF * jnp.sqrt(squares) * cons[5] - DEST_COEF * cons[0] * ratio * ratio
        rates = [-net[f] * half_inverse for f in range(FIELDS)]
        rates[5] = rates[5] + source
        store(slot, cons, rates)

    for slot in range(SLOTS):
        if slot == 0:
            one(slot)
        else:
            pl.when(slot < counts_ref[0, 0])(lambda slot=slot: one(slot))


def first_kernel(dev_count, axis, links_ref, counts_ref, metric_ref, state_ref, *refs):
    send_refs, plan_ref, limits_ref = refs[:4], refs[4], refs[5]
    table_jk, table_i, mask_ref = refs[6:]
    make_plan(links_ref, lax.axis_index(axis), dev_count, plan_ref, mask_ref)
    limit = None
    for slot in range(SLOTS):
        cons = [state_ref[slot, f] for f in range(FIELDS)]
        write_edges(cons, slot, table_jk, table_i)
        normals, volume = geometry(metric_ref, slot)
        _, velocity, _, sound = primitives(cons)
        total = None
        area = None
        for d in range(3):
            normal_vel = normals[d][0] * velocity[0] + normals[d][1] * velocity[1] + normals[d][2] * velocity[2]
            total = jnp.abs(normal_vel) if total is None else total + jnp.abs(normal_vel)
            one_area = area_of([splat(normals[d][e], (1, 1)) for e in range(3)])
            area = one_area if area is None else area + one_area
        total = total + sound * area
        own = COURANT * splat(volume, (1, 1)) / jnp.max(total, axis=(0, 1), keepdims=True)
        limit = own if limit is None else jnp.where(slot < counts_ref[0, 0], jnp.minimum(limit, own), limit)
    limits_ref[...] = jnp.broadcast_to(limit, limits_ref.shape)
    write_sends(table_jk, table_i, plan_ref, send_refs)


def fill_tables(received, table_jk, table_i):
    for n in range(len(OFFSETS)):
        for f in range(FIELDS):
            table_jk[SLOTS + n, f] = received[n](f)
        for b in range(2):
            at = 8 * (2 * SLOTS + n)
            table_i[b, at : at + 8, :] = received[n](6 + b)


def second_kernel(links_ref, counts_ref, metric_ref, inflow_ref, plan_ref, state_ref, distance_ref, *refs):
    received = refs[:4]
    rate_ref, send_refs = refs[4], refs[5:9]
    table_jk, table_i, ghost_i, edge_i = refs[9:]
    for slot in range(SLOTS):
        write_edges([state_ref[slot, f] for f in range(FIELDS)], slot, table_jk, table_i)
    fill_tables([lambda k, n=n: received[n][k] for n in range(4)], table_jk, table_i)

    def store(slot, cons, rates):
        for f in range(FIELDS):
            rate_ref[slot, f] = rates[f]

    section(
        lambda slot: [state_ref[slot, f] for f in range(FIELDS)],
        distance_ref, links_ref, counts_ref, metric_ref, inflow_ref, plan_ref, table_jk, table_i, ghost_i, edge_i, store,
    )
    for slot in range(SLOTS):
        def edges(slot=slot):
            write_edges([rate_ref[slot, f] for f in range(FIELDS)], slot, table_jk, table_i)

        if slot == 0:
            edges()
        else:
            pl.when(slot < counts_ref[0, 0])(edges)
    write_sends(table_jk, table_i, plan_ref, send_refs)


def third_kernel(links_ref, counts_ref, metric_ref, inflow_ref, plan_ref, state_ref, distance_ref, rate_ref, *refs):
    first, second, limits_ref = refs[:4], refs[4:8], refs[8]
    tendency_ref, step_ref = refs[9:11]
    table_jk, table_i, ghost_i, edge_i, middle_ref = refs[11:]
    step = jnp.min(limits_ref[...], axis=(0, 1), keepdims=True)
    step_ref[...] = step
    fill_tables([lambda k, n=n: first[n][k] + step * second[n][k] for n in range(4)], table_jk, table_i)
    for slot in range(SLOTS):
        def edges(slot=slot):
            middle = [state_ref[slot, f] + step * rate_ref[slot, f] for f in range(FIELDS)]
            for f in range(FIELDS):
                middle_ref[slot, f] = middle[f]
            write_edges(middle, slot, table_jk, table_i)

        if slot == 0:
            edges()
        else:
            pl.when(slot < counts_ref[0, 0])(edges)

    def store(slot, cons, rates):
        for f in range(FIELDS):
            tendency_ref[slot, f] = 0.5 * (rate_ref[slot, f] + rates[f])

    section(
        lambda slot: [middle_ref[slot, f] for f in range(FIELDS)],
        distance_ref, links_ref, counts_ref, metric_ref, inflow_ref, plan_ref, table_jk, table_i, ghost_i, edge_i, store,
    )
    for slot in range(1, SLOTS):
        @pl.when(slot >= counts_ref[0, 0])
        def _(slot=slot):
            for f in range(FIELDS):
                tendency_ref[slot, f] = jnp.zeros((NI, NJ * NK), f32)


def in_smem():
    return pl.BlockSpec(memory_space=pltpu.SMEM)


def in_vmem():
    return pl.BlockSpec(memory_space=pltpu.VMEM)


TABLES = (
    pltpu.VMEM((SLOTS + 4, FIELDS, 8, LANES), f32),
    pltpu.VMEM((2, 8 * (2 * SLOTS + 4), LANES), f32),
)
SCRATCH = TABLES + (pltpu.VMEM((2, 64, LANES), f32), pltpu.VMEM((9, 8, 2 * LANES), f32))


def body(state, wall_dist, block_metric, inflow, counts, links):
    axis = "blk"
    dev_count = lax.axis_size(axis)
    links = jnp.transpose(links, (0, 2, 1))
    counts = counts.reshape(1, 1)
    send = pltpu.VMEM(SEND, f32)
    block = pltpu.VMEM(state.shape, f32)

    def near_core(array):
        return pltpu.with_memory_space_constraint(array, pltpu.VMEM)

    state, wall_dist = near_core(state), near_core(wall_dist)

    *sends, plan, limits = pl.pallas_call(
        lambda *refs: first_kernel(dev_count, axis, *refs),
        out_shape=[send] * 4 + [jax.ShapeDtypeStruct((PLAN,), i32), pltpu.VMEM((dev_count, LANES), f32)],
        in_specs=[in_smem()] * 3 + [in_vmem()],
        out_specs=[in_vmem()] * 4 + [in_smem(), in_vmem()],
        scratch_shapes=TABLES + (pltpu.SMEM((16,), i32),),
        name="faces",
    )(links, counts, block_metric, state)

    def exchanged(arrays):
        result = []
        for array, offset in zip(reversed(arrays), OFFSETS):
            pairs = [((p + offset) % dev_count, p) for p in range(dev_count)]
            result.append(lax.ppermute(array, axis, pairs))
        return result

    limits = lax.all_to_all(limits, axis, 0, 0, tiled=True)
    first = exchanged(sends)
    rate, *sends_two = pl.pallas_call(
        second_kernel,
        out_shape=[block] + [send] * 4,
        in_specs=[in_smem()] * 5 + [in_vmem()] * 6,
        out_specs=[in_vmem()] * 5,
        scratch_shapes=SCRATCH,
        name="rate_one",
    )(links, counts, block_metric, inflow, plan, state, wall_dist, *map(near_core, first))

    second = exchanged(sends_two)

    tendency, step = pl.pallas_call(
        third_kernel,
        out_shape=[jax.ShapeDtypeStruct(state.shape, f32), jax.ShapeDtypeStruct((1, 1), f32)],
        in_specs=[in_smem()] * 5 + [in_vmem()] * 12,
        out_specs=[in_vmem()] * 2,
        scratch_shapes=SCRATCH + (pltpu.VMEM(state.shape, f32),),
        name="rate_two",
    )(links, counts, block_metric, inflow, plan, state, wall_dist, near_core(rate), *map(near_core, first), *map(near_core, second), near_core(limits))
    return tendency, step[0, 0]


def solution(mesh):
    return jax.shard_map(
        body,
        mesh=mesh,
        in_specs=(
            P("blk", None, None, None),
            P("blk", None, None),
            P("blk", None),
            P(),
            P("blk"),
            P("blk", None, None),
        ),
        out_specs=(P("blk", None, None, None), P()),
        check_vma=False,
    )
```

profile of v0, /device:TPU:1, one launch (start us, length us, event | category | flops | bytes accessed | tf_op | source)
XLA Modules:
  0.0 49.6 jit_solution(18148425901944339691)
XLA Ops:
  1.3 0.0 copy-start
  1.3 1.0 %copy-done = f32[3,6,16,256]{3,2,1,0:T(8,128)S(1)} copy-done((f32[3,6,16,256]{3,2,1,0:T(8,128)S(1)}, f32[3,6,16,256]{3,2,1,0:T(8,128)}, u32[]{:S(2)}) %copy-start) | copy-done | bytes 294936
  2.2 2.0 %faces.1 = (f32[8,8,128]{2,1,0:T(8,128)S(1)}, f32[8,8,128]{2,1,0:T(8,128)S(1)}, f32[8,8,128]{2,1,0:T(8,128)S(1)}, f32[8,8,128]{2,1,0:T(8,128)S(1)}, s32[128]{0:T(128)}, /*index=5*/f32[256,128]{1,0:T(8,128)}) custom-call(s32[3,4,6]{2,1,0:T(4,128)} %bitcast.11, s32[1,1]{1,0:T(1,128)} %bitcast.7.refs_1_, f32[3,10]{1,0:T(4,128)} %metric_ref.3, ...), custom_call_target="tpu_custom_call" | custom-call | tf_op jit(solution)/shard_map/faces/pallas_call | solution.py:500
  4.3 0.0 copy-start.1
  4.3 15.7 %all-to-all-start = ((f32[256,1,128]{2,1,0:T(1,128)}), f32[256,1,128]{2,1,0:T(1,128)S(1)}, u32[]{:S(2)}, u32[]{:S(2)}) async-start(f32[256,1,128]{2,1,0:T(1,128)} %bitcast.3), calls=%async_computation | async-start | bytes 262144 | tf_op jit(solution)/shard_map/all_to_all | solution.py:516
  19.9 1.4 %collective-permute-start = (f32[8,8,128]{2,1,0:T(8,128)S(1)}, f32[8,8,128]{2,1,0:T(8,128)S(1)}, u32[]{:S(2)}, u32[]{:S(2)}) collective-permute-start(f32[8,8,128]{2,1,0:T(8,128)S(1)} %get-tuple-element.16), channel_id=1, source_target_pairs={{254,0},{255,1},{0,2},{1,3},{2,4},{3,5},{4,6},{5,7},{6,8},{7,9},{8... | collective-permute-start | bytes 98312 | tf_op jit(solution)/shard_map/ppermute | solution.py:513
  21.4 1.7 %collective-permute-start.1 = (f32[8,8,128]{2,1,0:T(8,128)S(1)}, f32[8,8,128]{2,1,0:T(8,128)S(1)}, u32[]{:S(2)}, u32[]{:S(2)}) collective-permute-start(f32[8,8,128]{2,1,0:T(8,128)S(1)} %get-tuple-element.17), channel_id=1, source_target_pairs={{255,0},{0,1},{1,2},{2,3},{3,4},{4,5},{5,6},{6,7},{7,8},{8,9},{9,1... | collective-permute-start | bytes 98312 | tf_op jit(solution)/shard_map/ppermute | solution.py:513
  23.1 0.0 collective-permute-start.2
  23.1 6.3 %collective-permute-start.3 = (f32[8,8,128]{2,1,0:T(8,128)S(1)}, f32[8,8,128]{2,1,0:T(8,128)S(1)}, u32[]{:S(2)}, u32[]{:S(2)}) collective-permute-start(f32[8,8,128]{2,1,0:T(8,128)S(1)} %get-tuple-element.19), channel_id=1, source_target_pairs={{2,0},{3,1},{4,2},{5,3},{6,4},{7,5},{8,6},{9,7},{10,8},{11,9},{12,... | collective-permute-start | bytes 98312 | tf_op jit(solution)/shard_map/ppermute | solution.py:513
  29.4 2.5 %collective-permute-done.refs_0_ = f32[8,8,128]{2,1,0:T(8,128)S(1)} collective-permute-done((f32[8,8,128]{2,1,0:T(8,128)S(1)}, f32[8,8,128]{2,1,0:T(8,128)S(1)}, u32[]{:S(2)}, u32[]{:S(2)}) %collective-permute-start) | collective-permute-done | bytes 32800 | tf_op jit(solution)/shard_map/ppermute | solution.py:513
  31.9 0.0 collective-permute-done.1.refs_1_
  31.9 0.0 collective-permute-done.2.refs_2_
  31.9 0.0 collective-permute-done.3.refs_3_
  31.9 0.0 copy-done.1
  31.9 3.2 %rate_one.1 = (f32[3,6,16,256]{3,2,1,0:T(8,128)S(1)}, f32[8,8,128]{2,1,0:T(8,128)S(1)}, f32[8,8,128]{2,1,0:T(8,128)S(1)}, f32[8,8,128]{2,1,0:T(8,128)S(1)}, f32[8,8,128]{2,1,0:T(8,128)S(1)}) custom-call(s32[3,4,6]{2,1,0:T(4,128)} %bitcast.12, s32[1,1]{1,0:T(1,128)} %bitcast.8.counts_ref, f32[3,10]{1,0:T(4,128)} %metric_ref.3, f32[6]{0:T(128)} %inflow_ref.3, ...), custom_call_target="tpu_custom_call" | custom-call | tf_op jit(solution)/shard_map/rate_one/pallas_call | solution.py:518
  35.1 0.1 collective-permute-start.4
  35.2 0.9 %collective-permute-start.5 = (f32[8,8,128]{2,1,0:T(8,128)S(1)}, f32[8,8,128]{2,1,0:T(8,128)S(1)}, u32[]{:S(2)}, u32[]{:S(2)}) collective-permute-start(f32[8,8,128]{2,1,0:T(8,128)S(1)} %get-tuple-element.22), channel_id=1, source_target_pairs={{255,0},{0,1},{1,2},{2,3},{3,4},{4,5},{5,6},{6,7},{7,8},{8,9},{9,1... | collective-permute-start | bytes 98312 | tf_op jit(solution)/shard_map/ppermute | solution.py:513
  36.1 0.3 collective-permute-start.6
  36.4 8.4 %collective-permute-start.7 = (f32[8,8,128]{2,1,0:T(8,128)S(1)}, f32[8,8,128]{2,1,0:T(8,128)S(1)}, u32[]{:S(2)}, u32[]{:S(2)}) collective-permute-start(f32[8,8,128]{2,1,0:T(8,128)S(1)} %get-tuple-element.24), channel_id=1, source_target_pairs={{2,0},{3,1},{4,2},{5,3},{6,4},{7,5},{8,6},{9,7},{10,8},{11,9},{12,... | collective-permute-start | bytes 98312 | tf_op jit(solution)/shard_map/ppermute | solution.py:513
  44.8 0.0 collective-permute-done.4.refs_4_
  44.8 0.0 collective-permute-done.5.refs_5_
  44.8 0.0 collective-permute-done.6.refs_6_
  44.8 1.0 %collective-permute-done.7.refs_7_ = f32[8,8,128]{2,1,0:T(8,128)S(1)} collective-permute-done((f32[8,8,128]{2,1,0:T(8,128)S(1)}, f32[8,8,128]{2,1,0:T(8,128)S(1)}, u32[]{:S(2)}, u32[]{:S(2)}) %collective-permute-start.7) | collective-permute-done | bytes 32800 | tf_op jit(solution)/shard_map/ppermute | solution.py:513
  45.8 0.0 all-to-all-done
  45.8 3.7 %rate_two.1 = (f32[3,6,16,256]{3,2,1,0:T(8,128)}, f32[1,1]{1,0:T(1,128)}) custom-call(s32[3,4,6]{2,1,0:T(4,128)} %bitcast.13, s32[1,1]{1,0:T(1,128)} %bitcast.9.counts_ref, f32[3,10]{1,0:T(4,128)} %metric_ref.3, f32[6]{0:T(128)} %inflow_ref.3, s32[128]{0:T(128)} %get-tuple-element.15.plan_ref, f32[3,6,16,256]{3,2,1,0:T(8,128)S(1)} %copy-done, ...), custom_call_target="tpu_custom_call" | custom-call | tf_op jit(solution)/shard_map/rate_two/pallas_call | solution.py:529
Async XLA Ops:
  1.3 1.0 %copy-start = (f32[3,6,16,256]{3,2,1,0:T(8,128)S(1)}, f32[3,6,16,256]{3,2,1,0:T(8,128)}, u32[]{:S(2)}) copy-start(f32[3,6,16,256]{3,2,1,0:T(8,128)} %state_ref.3) | copy-start | bytes 884740
  4.3 27.6 %copy-start.1 = (f32[3,16,256]{2,1,0:T(8,128)S(1)}, f32[3,16,256]{2,1,0:T(8,128)}, u32[]{:S(2)}) copy-start(f32[3,16,256]{2,1,0:T(8,128)} %distance_ref.3) | copy-start | bytes 147460
  4.3 41.5 %all-to-all-start = ((f32[256,1,128]{2,1,0:T(1,128)}), f32[256,1,128]{2,1,0:T(1,128)S(1)}, u32[]{:S(2)}, u32[]{:S(2)}) async-start(f32[256,1,128]{2,1,0:T(1,128)} %bitcast.3), calls=%async_computation | async-start | bytes 262144 | tf_op jit(solution)/shard_map/all_to_all | solution.py:516
  19.9 11.9 %collective-permute-start = (f32[8,8,128]{2,1,0:T(8,128)S(1)}, f32[8,8,128]{2,1,0:T(8,128)S(1)}, u32[]{:S(2)}, u32[]{:S(2)}) collective-permute-start(f32[8,8,128]{2,1,0:T(8,128)S(1)} %get-tuple-element.16), channel_id=1, source_target_pairs={{254,0},{255,1},{0,2},{1,3},{2,4},{3,5},{4,6},{5,7},{6,8},{7,9},{8... | collective-permute-start | bytes 98312 | tf_op jit(solution)/shard_map/ppermute | solution.py:513
  21.4 10.5 %collective-permute-start.1 = (f32[8,8,128]{2,1,0:T(8,128)S(1)}, f32[8,8,128]{2,1,0:T(8,128)S(1)}, u32[]{:S(2)}, u32[]{:S(2)}) collective-permute-start(f32[8,8,128]{2,1,0:T(8,128)S(1)} %get-tuple-element.17), channel_id=1, source_target_pairs={{255,0},{0,1},{1,2},{2,3},{3,4},{4,5},{5,6},{6,7},{7,8},{8,9},{9,1... | collective-permute-start | bytes 98312 | tf_op jit(solution)/shard_map/ppermute | solution.py:513
  23.1 8.7 %collective-permute-start.2 = (f32[8,8,128]{2,1,0:T(8,128)S(1)}, f32[8,8,128]{2,1,0:T(8,128)S(1)}, u32[]{:S(2)}, u32[]{:S(2)}) collective-permute-start(f32[8,8,128]{2,1,0:T(8,128)S(1)} %get-tuple-element.18), channel_id=1, source_target_pairs={{1,0},{2,1},{3,2},{4,3},{5,4},{6,5},{7,6},{8,7},{9,8},{10,9},{11,1... | collective-permute-start | bytes 98312 | tf_op jit(solution)/shard_map/ppermute | solution.py:513
  23.1 8.7 %collective-permute-start.3 = (f32[8,8,128]{2,1,0:T(8,128)S(1)}, f32[8,8,128]{2,1,0:T(8,128)S(1)}, u32[]{:S(2)}, u32[]{:S(2)}) collective-permute-start(f32[8,8,128]{2,1,0:T(8,128)S(1)} %get-tuple-element.19), channel_id=1, source_target_pairs={{2,0},{3,1},{4,2},{5,3},{6,4},{7,5},{8,6},{9,7},{10,8},{11,9},{12,... | collective-permute-start | bytes 98312 | tf_op jit(solution)/shard_map/ppermute | solution.py:513
  35.1 9.7 %collective-permute-start.4 = (f32[8,8,128]{2,1,0:T(8,128)S(1)}, f32[8,8,128]{2,1,0:T(8,128)S(1)}, u32[]{:S(2)}, u32[]{:S(2)}) collective-permute-start(f32[8,8,128]{2,1,0:T(8,128)S(1)} %get-tuple-element.21), channel_id=1, source_target_pairs={{254,0},{255,1},{0,2},{1,3},{2,4},{3,5},{4,6},{5,7},{6,8},{7,9},{8... | collective-permute-start | bytes 98312 | tf_op jit(solution)/shard_map/ppermute | solution.py:513
  35.2 9.6 %collective-permute-start.5 = (f32[8,8,128]{2,1,0:T(8,128)S(1)}, f32[8,8,128]{2,1,0:T(8,128)S(1)}, u32[]{:S(2)}, u32[]{:S(2)}) collective-permute-start(f32[8,8,128]{2,1,0:T(8,128)S(1)} %get-tuple-element.22), channel_id=1, source_target_pairs={{255,0},{0,1},{1,2},{2,3},{3,4},{4,5},{5,6},{6,7},{7,8},{8,9},{9,1... | collective-permute-start | bytes 98312 | tf_op jit(solution)/shard_map/ppermute | solution.py:513
  36.1 8.7 %collective-permute-start.6 = (f32[8,8,128]{2,1,0:T(8,128)S(1)}, f32[8,8,128]{2,1,0:T(8,128)S(1)}, u32[]{:S(2)}, u32[]{:S(2)}) collective-permute-start(f32[8,8,128]{2,1,0:T(8,128)S(1)} %get-tuple-element.23), channel_id=1, source_target_pairs={{1,0},{2,1},{3,2},{4,3},{5,4},{6,5},{7,6},{8,7},{9,8},{10,9},{11,1... | collective-permute-start | bytes 98312 | tf_op jit(solution)/shard_map/ppermute | solution.py:513
  36.4 9.4 %collective-permute-start.7 = (f32[8,8,128]{2,1,0:T(8,128)S(1)}, f32[8,8,128]{2,1,0:T(8,128)S(1)}, u32[]{:S(2)}, u32[]{:S(2)}) collective-permute-start(f32[8,8,128]{2,1,0:T(8,128)S(1)} %get-tuple-element.24), channel_id=1, source_target_pairs={{2,0},{3,1},{4,2},{5,3},{6,4},{7,5},{8,6},{9,7},{10,8},{11,9},{12,... | collective-permute-start | bytes 98312 | tf_op jit(solution)/shard_map/ppermute | solution.py:513
where the time goes:
time: 49.9 us; the launch traced here: 49.6 us
  starting transfers between devices  34.8 us (70%)
  Pallas kernels  8.99 us (18%)
  waiting for transfers between devices  3.49 us (7%)
  between operations  1.34 us (3%)
  local copies, waits for them, and re-layouts  0.96 us (2%)
    ppermute x8, starting transfers between devices, exchanged(): result.append(lax.ppermute(array, axis, pairs))  19.1 us
    all_to_all x1, starting transfers between devices, body(): limits = lax.all_to_all(limits, axis, 0, 0, tiled=True)  15.7 us
    pallas_call x1, Pallas kernels, body(): pl.pallas_call(third_kernel, out_shape=[jax.ShapeDtypeStruct(state.shape,...  3.73 us
    ppermute x8, waiting for transfers between devices, exchanged(): result.append(lax.ppermute(array, axis, pairs))  3.49 us
    pallas_call x1, Pallas kernels, body(): pl.pallas_call(second_kernel, out_shape=[block] + [send] * 4, in_specs=[i...  3.23 us
    pallas_call x1, Pallas kernels, body(): pl.pallas_call(lambda *refs: first_kernel(dev_count, axis, *refs), out_sh...  2.03 us
  transfers between devices with their start and end apart: 9, of which 2 were waited for; matrix products, arithmetic and copies ran while one was open for 0% of the time, Pallas kernels for 7%

commit v1 on v0

--- a/solution.py
+++ b/solution.py
@@ -495,7 +495,7 @@
     def near_core(array):
         return pltpu.with_memory_space_constraint(array, pltpu.VMEM)
 
-    state, wall_dist = near_core(state), near_core(wall_dist)
+    state_near, wall_dist = near_core(state), near_core(wall_dist)
 
     *sends, plan, limits = pl.pallas_call(
         lambda *refs: first_kernel(dev_count, axis, *refs),
@@ -522,7 +522,7 @@
         out_specs=[in_vmem()] * 5,
         scratch_shapes=SCRATCH,
         name="rate_one",
-    )(links, counts, block_metric, inflow, plan, state, wall_dist, *map(near_core, first))
+    )(links, counts, block_metric, inflow, plan, state_near, wall_dist, *map(near_core, first))
 
     second = exchanged(sends_two)
 
@@ -533,7 +533,7 @@
         out_specs=[in_vmem()] * 2,
         scratch_shapes=SCRATCH + (pltpu.VMEM(state.shape, f32),),
         name="rate_two",
-    )(links, counts, block_metric, inflow, plan, state, wall_dist, near_core(rate), *map(near_core, first), *map(near_core, second), near_core(limits))
+    )(links, counts, block_metric, inflow, plan, state_near, wall_dist, near_core(rate), *map(near_core, first), *map(near_core, second), near_core(limits))
     return tendency, step[0, 0]
 
 

time: 49.9 us -> 49.1 us (0.984)
  local copies, waits for them, and re-layouts: 0.96 us -> 0.01 us
    unnamed x4, local copies, waits for them, and re-layouts: 0.96 us -> 0.01 us
where the time goes in v1:
time: 49.1 us; the launch traced here: 48.8 us
  starting transfers between devices  34.8 us (71%)
  Pallas kernels  9.18 us (19%)
  waiting for transfers between devices  3.49 us (7%)
  between operations  1.4 us (3%)
    ppermute x8, starting transfers between devices, exchanged(): result.append(lax.ppermute(array, axis, pairs))  19.1 us
    all_to_all x1, starting transfers between devices, body(): limits = lax.all_to_all(limits, axis, 0, 0, tiled=True)  15.7 us
    pallas_call x1, Pallas kernels, body(): pl.pallas_call(third_kernel, out_shape=[jax.ShapeDtypeStruct(state.shape,...  3.73 us
    ppermute x8, waiting for transfers between devices, exchanged(): result.append(lax.ppermute(array, axis, pairs))  3.49 us
    pallas_call x1, Pallas kernels, body(): pl.pallas_call(second_kernel, out_shape=[block] + [send] * 4, in_specs=[i...  3.23 us
    pallas_call x1, Pallas kernels, body(): pl.pallas_call(lambda *refs: first_kernel(dev_count, axis, *refs), out_sh...  2.21 us
  transfers between devices with their start and end apart: 9, of which 2 were waited for; matrix products, arithmetic and copies ran while one was open for 0% of the time, Pallas kernels for 7%

profile of v1, /device:TPU:1, one launch (start us, length us, event | category | flops | bytes accessed | tf_op | source)
XLA Modules:
  0.0 48.8 jit_solution(2065347321256229051)
XLA Ops:
  0.6 0.0 copy-start
  1.3 2.2 %faces.1 = (f32[8,8,128]{2,1,0:T(8,128)S(1)}, f32[8,8,128]{2,1,0:T(8,128)S(1)}, f32[8,8,128]{2,1,0:T(8,128)S(1)}, f32[8,8,128]{2,1,0:T(8,128)S(1)}, s32[128]{0:T(128)}, /*index=5*/f32[256,128]{1,0:T(8,128)}) custom-call(s32[3,4,6]{2,1,0:T(4,128)} %bitcast.11, s32[1,1]{1,0:T(1,128)} %bitcast.7.refs_1_, f32[3,10]{1,0:T(4,128)} %metric_ref.3, ...), custom_call_target="tpu_custom_call" | custom-call | tf_op jit(solution)/shard_map/faces/pallas_call | solution.py:500
  3.6 0.0 copy-start.1
  3.6 15.7 %all-to-all-start = ((f32[256,1,128]{2,1,0:T(1,128)}), f32[256,1,128]{2,1,0:T(1,128)S(1)}, u32[]{:S(2)}, u32[]{:S(2)}) async-start(f32[256,1,128]{2,1,0:T(1,128)} %bitcast.3), calls=%async_computation | async-start | bytes 262144 | tf_op jit(solution)/shard_map/all_to_all | solution.py:516
  19.2 1.4 %collective-permute-start = (f32[8,8,128]{2,1,0:T(8,128)S(1)}, f32[8,8,128]{2,1,0:T(8,128)S(1)}, u32[]{:S(2)}, u32[]{:S(2)}) collective-permute-start(f32[8,8,128]{2,1,0:T(8,128)S(1)} %get-tuple-element.16), channel_id=1, source_target_pairs={{254,0},{255,1},{0,2},{1,3},{2,4},{3,5},{4,6},{5,7},{6,8},{7,9},{8... | collective-permute-start | bytes 98312 | tf_op jit(solution)/shard_map/ppermute | solution.py:513
  20.7 1.7 %collective-permute-start.1 = (f32[8,8,128]{2,1,0:T(8,128)S(1)}, f32[8,8,128]{2,1,0:T(8,128)S(1)}, u32[]{:S(2)}, u32[]{:S(2)}) collective-permute-start(f32[8,8,128]{2,1,0:T(8,128)S(1)} %get-tuple-element.17), channel_id=1, source_target_pairs={{255,0},{0,1},{1,2},{2,3},{3,4},{4,5},{5,6},{6,7},{7,8},{8,9},{9,1... | collective-permute-start | bytes 98312 | tf_op jit(solution)/shard_map/ppermute | solution.py:513
  22.4 0.0 collective-permute-start.2
  22.4 6.3 %collective-permute-start.3 = (f32[8,8,128]{2,1,0:T(8,128)S(1)}, f32[8,8,128]{2,1,0:T(8,128)S(1)}, u32[]{:S(2)}, u32[]{:S(2)}) collective-permute-start(f32[8,8,128]{2,1,0:T(8,128)S(1)} %get-tuple-element.19), channel_id=1, source_target_pairs={{2,0},{3,1},{4,2},{5,3},{6,4},{7,5},{8,6},{9,7},{10,8},{11,9},{12,... | collective-permute-start | bytes 98312 | tf_op jit(solution)/shard_map/ppermute | solution.py:513
  28.7 2.5 %collective-permute-done.refs_0_ = f32[8,8,128]{2,1,0:T(8,128)S(1)} collective-permute-done((f32[8,8,128]{2,1,0:T(8,128)S(1)}, f32[8,8,128]{2,1,0:T(8,128)S(1)}, u32[]{:S(2)}, u32[]{:S(2)}) %collective-permute-start) | collective-permute-done | bytes 32800 | tf_op jit(solution)/shard_map/ppermute | solution.py:513
  31.1 0.0 collective-permute-done.1.refs_1_
  31.1 0.0 collective-permute-done.2.refs_2_
  31.1 0.0 collective-permute-done.3.refs_3_
  31.2 0.0 copy-done
  31.2 0.0 copy-done.1
  31.2 3.2 %rate_one.1 = (f32[3,6,16,256]{3,2,1,0:T(8,128)S(1)}, f32[8,8,128]{2,1,0:T(8,128)S(1)}, f32[8,8,128]{2,1,0:T(8,128)S(1)}, f32[8,8,128]{2,1,0:T(8,128)S(1)}, f32[8,8,128]{2,1,0:T(8,128)S(1)}) custom-call(s32[3,4,6]{2,1,0:T(4,128)} %bitcast.12, s32[1,1]{1,0:T(1,128)} %bitcast.8.counts_ref, f32[3,10]{1,0:T(4,128)} %metric_ref.3, f32[6]{0:T(128)} %inflow_ref.3, ...), custom_call_target="tpu_custom_call" | custom-call | tf_op jit(solution)/shard_map/rate_one/pallas_call | solution.py:518
  34.4 0.1 collective-permute-start.4
  34.5 0.8 %collective-permute-start.5 = (f32[8,8,128]{2,1,0:T(8,128)S(1)}, f32[8,8,128]{2,1,0:T(8,128)S(1)}, u32[]{:S(2)}, u32[]{:S(2)}) collective-permute-start(f32[8,8,128]{2,1,0:T(8,128)S(1)} %get-tuple-element.22), channel_id=1, source_target_pairs={{255,0},{0,1},{1,2},{2,3},{3,4},{4,5},{5,6},{6,7},{7,8},{8,9},{9,1... | collective-permute-start | bytes 98312 | tf_op jit(solution)/shard_map/ppermute | solution.py:513
  35.3 0.3 collective-permute-start.6
  35.7 8.4 %collective-permute-start.7 = (f32[8,8,128]{2,1,0:T(8,128)S(1)}, f32[8,8,128]{2,1,0:T(8,128)S(1)}, u32[]{:S(2)}, u32[]{:S(2)}) collective-permute-start(f32[8,8,128]{2,1,0:T(8,128)S(1)} %get-tuple-element.24), channel_id=1, source_target_pairs={{2,0},{3,1},{4,2},{5,3},{6,4},{7,5},{8,6},{9,7},{10,8},{11,9},{12,... | collective-permute-start | bytes 98312 | tf_op jit(solution)/shard_map/ppermute | solution.py:513
  44.1 0.0 collective-permute-done.4.refs_4_
  44.1 0.0 collective-permute-done.5.refs_5_
  44.1 0.0 collective-permute-done.6.refs_6_
  44.1 1.0 %collective-permute-done.7.refs_7_ = f32[8,8,128]{2,1,0:T(8,128)S(1)} collective-permute-done((f32[8,8,128]{2,1,0:T(8,128)S(1)}, f32[8,8,128]{2,1,0:T(8,128)S(1)}, u32[]{:S(2)}, u32[]{:S(2)}) %collective-permute-start.7) | collective-permute-done | bytes 32800 | tf_op jit(solution)/shard_map/ppermute | solution.py:513
  45.1 0.0 all-to-all-done
  45.1 3.7 %rate_two.1 = (f32[3,6,16,256]{3,2,1,0:T(8,128)}, f32[1,1]{1,0:T(1,128)}) custom-call(s32[3,4,6]{2,1,0:T(4,128)} %bitcast.13, s32[1,1]{1,0:T(1,128)} %bitcast.9.counts_ref, f32[3,10]{1,0:T(4,128)} %metric_ref.3, f32[6]{0:T(128)} %inflow_ref.3, s32[128]{0:T(128)} %get-tuple-element.15.plan_ref, f32[3,6,16,256]{3,2,1,0:T(8,128)S(1)} %copy-done, ...), custom_call_target="tpu_custom_call" | custom-call | tf_op jit(solution)/shard_map/rate_two/pallas_call | solution.py:529
Async XLA Ops:
  0.6 30.5 %copy-start = (f32[3,6,16,256]{3,2,1,0:T(8,128)S(1)}, f32[3,6,16,256]{3,2,1,0:T(8,128)}, u32[]{:S(2)}) copy-start(f32[3,6,16,256]{3,2,1,0:T(8,128)} %state_ref.3) | copy-start | bytes 884740
  3.6 27.6 %copy-start.1 = (f32[3,16,256]{2,1,0:T(8,128)S(1)}, f32[3,16,256]{2,1,0:T(8,128)}, u32[]{:S(2)}) copy-start(f32[3,16,256]{2,1,0:T(8,128)} %distance_ref.3) | copy-start | bytes 147460
  3.6 41.5 %all-to-all-start = ((f32[256,1,128]{2,1,0:T(1,128)}), f32[256,1,128]{2,1,0:T(1,128)S(1)}, u32[]{:S(2)}, u32[]{:S(2)}) async-start(f32[256,1,128]{2,1,0:T(1,128)} %bitcast.3), calls=%async_computation | async-start | bytes 262144 | tf_op jit(solution)/shard_map/all_to_all | solution.py:516
  19.2 11.9 %collective-permute-start = (f32[8,8,128]{2,1,0:T(8,128)S(1)}, f32[8,8,128]{2,1,0:T(8,128)S(1)}, u32[]{:S(2)}, u32[]{:S(2)}) collective-permute-start(f32[8,8,128]{2,1,0:T(8,128)S(1)} %get-tuple-element.16), channel_id=1, source_target_pairs={{254,0},{255,1},{0,2},{1,3},{2,4},{3,5},{4,6},{5,7},{6,8},{7,9},{8... | collective-permute-start | bytes 98312 | tf_op jit(solution)/shard_map/ppermute | solution.py:513
  20.7 10.5 %collective-permute-start.1 = (f32[8,8,128]{2,1,0:T(8,128)S(1)}, f32[8,8,128]{2,1,0:T(8,128)S(1)}, u32[]{:S(2)}, u32[]{:S(2)}) collective-permute-start(f32[8,8,128]{2,1,0:T(8,128)S(1)} %get-tuple-element.17), channel_id=1, source_target_pairs={{255,0},{0,1},{1,2},{2,3},{3,4},{4,5},{5,6},{6,7},{7,8},{8,9},{9,1... | collective-permute-start | bytes 98312 | tf_op jit(solution)/shard_map/ppermute | solution.py:513
  22.4 8.7 %collective-permute-start.2 = (f32[8,8,128]{2,1,0:T(8,128)S(1)}, f32[8,8,128]{2,1,0:T(8,128)S(1)}, u32[]{:S(2)}, u32[]{:S(2)}) collective-permute-start(f32[8,8,128]{2,1,0:T(8,128)S(1)} %get-tuple-element.18), channel_id=1, source_target_pairs={{1,0},{2,1},{3,2},{4,3},{5,4},{6,5},{7,6},{8,7},{9,8},{10,9},{11,1... | collective-permute-start | bytes 98312 | tf_op jit(solution)/shard_map/ppermute | solution.py:513
  22.4 8.7 %collective-permute-start.3 = (f32[8,8,128]{2,1,0:T(8,128)S(1)}, f32[8,8,128]{2,1,0:T(8,128)S(1)}, u32[]{:S(2)}, u32[]{:S(2)}) collective-permute-start(f32[8,8,128]{2,1,0:T(8,128)S(1)} %get-tuple-element.19), channel_id=1, source_target_pairs={{2,0},{3,1},{4,2},{5,3},{6,4},{7,5},{8,6},{9,7},{10,8},{11,9},{12,... | collective-permute-start | bytes 98312 | tf_op jit(solution)/shard_map/ppermute | solution.py:513
  34.4 9.7 %collective-permute-start.4 = (f32[8,8,128]{2,1,0:T(8,128)S(1)}, f32[8,8,128]{2,1,0:T(8,128)S(1)}, u32[]{:S(2)}, u32[]{:S(2)}) collective-permute-start(f32[8,8,128]{2,1,0:T(8,128)S(1)} %get-tuple-element.21), channel_id=1, source_target_pairs={{254,0},{255,1},{0,2},{1,3},{2,4},{3,5},{4,6},{5,7},{6,8},{7,9},{8... | collective-permute-start | bytes 98312 | tf_op jit(solution)/shard_map/ppermute | solution.py:513
  34.5 9.6 %collective-permute-start.5 = (f32[8,8,128]{2,1,0:T(8,128)S(1)}, f32[8,8,128]{2,1,0:T(8,128)S(1)}, u32[]{:S(2)}, u32[]{:S(2)}) collective-permute-start(f32[8,8,128]{2,1,0:T(8,128)S(1)} %get-tuple-element.22), channel_id=1, source_target_pairs={{255,0},{0,1},{1,2},{2,3},{3,4},{4,5},{5,6},{6,7},{7,8},{8,9},{9,1... | collective-permute-start | bytes 98312 | tf_op jit(solution)/shard_map/ppermute | solution.py:513
  35.3 8.7 %collective-permute-start.6 = (f32[8,8,128]{2,1,0:T(8,128)S(1)}, f32[8,8,128]{2,1,0:T(8,128)S(1)}, u32[]{:S(2)}, u32[]{:S(2)}) collective-permute-start(f32[8,8,128]{2,1,0:T(8,128)S(1)} %get-tuple-element.23), channel_id=1, source_target_pairs={{1,0},{2,1},{3,2},{4,3},{5,4},{6,5},{7,6},{8,7},{9,8},{10,9},{11,1... | collective-permute-start | bytes 98312 | tf_op jit(solution)/shard_map/ppermute | solution.py:513
  35.7 9.4 %collective-permute-start.7 = (f32[8,8,128]{2,1,0:T(8,128)S(1)}, f32[8,8,128]{2,1,0:T(8,128)S(1)}, u32[]{:S(2)}, u32[]{:S(2)}) collective-permute-start(f32[8,8,128]{2,1,0:T(8,128)S(1)} %get-tuple-element.24), channel_id=1, source_target_pairs={{2,0},{3,1},{4,2},{5,3},{6,4},{7,5},{8,6},{9,7},{10,8},{11,9},{12,... | collective-permute-start | bytes 98312 | tf_op jit(solution)/shard_map/ppermute | solution.py:513

commit v2 on v1

--- a/solution.py
+++ b/solution.py
@@ -11,7 +11,7 @@
 SLOTS = 3
 FIELDS = 6
 LANES = 128
-OFFSETS = (-2, -1, 1, 2)
+SPACES = 4
 
 GAMMA = 1.4
 PROD_COEF = 0.1355
@@ -23,6 +23,7 @@
 PLAN = 128
 PLAN_I = 16
 PLAN_FACE = 32
+PLAN_VIA = 24
 
 f32 = jnp.float32
 i32 = jnp.int32
@@ -171,18 +172,28 @@
 
 
 def make_plan(links_ref, device, dev_count, plan_ref, mask_ref):
+    core = device & 1
+    odd_chip = lax.shift_right_logical(device, 1) & 1
+
     def entry(slot, face):
         code, block, other = links_ref[slot, 0, face], links_ref[slot, 1, face], links_ref[slot, 2, face]
         partner_dev = lax.div(block, SLOTS)
         away = lax.rem(partner_dev - device + dev_count, dev_count)
         space = jnp.where(
-            away == dev_count - 2, 0, jnp.where(away == dev_count - 1, 1, jnp.where(away == 1, 2, jnp.where(away == 2, 3, 4)))
+            away == 2,
+            odd_chip,
+            jnp.where(
+                away == dev_count - 2,
+                1 - odd_chip,
+                jnp.where(away == 1, 2 + core, jnp.where(away == dev_count - 1, 3 - core, 4)),
+            ),
         )
         space = jnp.where(code == 3, space, 4)
         return space, block - SLOTS * partner_dev, other
 
     for n in range(PLAN_I + 5):
         plan_ref[n] = 0
+    plan_ref[PLAN_VIA] = core ^ odd_chip
     for n in range(5):
         mask_ref[n] = 0
         mask_ref[8 + n] = 0
@@ -218,7 +229,8 @@
     group = lane // NK % 4
     base = (lane & 64) | (lane % NK)
     row = iota((8, LANES), 0)
-    for n in range(len(OFFSETS)):
+    for n in range(SPACES):
+        places = ((send_refs[0].at[0],), (send_refs[1].at[0],), (send_refs[2],), (send_refs[0].at[1], send_refs[1].at[1]))[n]
         chosen = []
         for q in range(3):
             source = plan_ref[3 * n + q]
@@ -226,12 +238,15 @@
             slot = lax.shift_right_logical(source, 2)
             chosen.append([pick(table_jk[slot, f], index, 1) for f in range(FIELDS)])
         for f in range(FIELDS):
-            send_refs[n][f] = jnp.where(group == 0, chosen[0][f], jnp.where(group == 1, chosen[1][f], chosen[2][f]))
+            value = jnp.where(group == 0, chosen[0][f], jnp.where(group == 1, chosen[1][f], chosen[2][f]))
+            for place in places:
+                place[f] = value
         at = pl.multiple_of(8 * plan_ref[PLAN_I + n], 8)
         first = table_i[0, pl.ds(at, 8), :]
         second = table_i[1, pl.ds(at, 8), :]
-        send_refs[n][6] = jnp.where(row < FIELDS, first, 0.0)
-        send_refs[n][7] = jnp.where(row < FIELDS, second, 0.0)
+        for place in places:
+            place[6] = jnp.where(row < FIELDS, first, 0.0)
+            place[7] = jnp.where(row < FIELDS, second, 0.0)
 
 
 def jk_ghosts(slot, table_jk, links_ref, plan_ref, far):
@@ -376,8 +391,8 @@
 
 
 def first_kernel(dev_count, axis, links_ref, counts_ref, metric_ref, state_ref, *refs):
-    send_refs, plan_ref, limits_ref = refs[:4], refs[4], refs[5]
-    table_jk, table_i, mask_ref = refs[6:]
+    send_refs, plan_ref, limits_ref = refs[:3], refs[3], refs[4]
+    table_jk, table_i, mask_ref = refs[5:]
     make_plan(links_ref, lax.axis_index(axis), dev_count, plan_ref, mask_ref)
     limit = None
     for slot in range(SLOTS):
@@ -399,8 +414,18 @@
     write_sends(table_jk, table_i, plan_ref, send_refs)
 
 
+def by_space(refs, plan_ref):
+    near, far, chip, near_passed, far_passed = refs
+    return [
+        lambda k: near[0, k],
+        lambda k: far[0, k],
+        lambda k: chip[k],
+        lambda k: jnp.where(plan_ref[PLAN_VIA] == 1, near_passed[1, k], far_passed[1, k]),
+    ]
+
+
 def fill_tables(received, table_jk, table_i):
-    for n in range(len(OFFSETS)):
+    for n in range(SPACES):
         for f in range(FIELDS):
             table_jk[SLOTS + n, f] = received[n](f)
         for b in range(2):
@@ -409,12 +434,12 @@
 
 
 def second_kernel(links_ref, counts_ref, metric_ref, inflow_ref, plan_ref, state_ref, distance_ref, *refs):
-    received = refs[:4]
-    rate_ref, send_refs = refs[4], refs[5:9]
+    received = by_space(refs[:5], plan_ref)
+    rate_ref, send_refs = refs[5], refs[6:9]
     table_jk, table_i, ghost_i, edge_i = refs[9:]
     for slot in range(SLOTS):
         write_edges([state_ref[slot, f] for f in range(FIELDS)], slot, table_jk, table_i)
-    fill_tables([lambda k, n=n: received[n][k] for n in range(4)], table_jk, table_i)
+    fill_tables(received, table_jk, table_i)
 
     def store(slot, cons, rates):
         for f in range(FIELDS):
@@ -436,12 +461,12 @@
 
 
 def third_kernel(links_ref, counts_ref, metric_ref, inflow_ref, plan_ref, state_ref, distance_ref, rate_ref, *refs):
-    first, second, limits_ref = refs[:4], refs[4:8], refs[8]
-    tendency_ref, step_ref = refs[9:11]
-    table_jk, table_i, ghost_i, edge_i, middle_ref = refs[11:]
+    first, second, limits_ref = by_space(refs[:5], plan_ref), by_space(refs[5:10], plan_ref), refs[10]
+    tendency_ref, step_ref = refs[11:13]
+    table_jk, table_i, ghost_i, edge_i, middle_ref = refs[13:]
     step = jnp.min(limits_ref[...], axis=(0, 1), keepdims=True)
     step_ref[...] = step
-    fill_tables([lambda k, n=n: first[n][k] + step * second[n][k] for n in range(4)], table_jk, table_i)
+    fill_tables([lambda k, n=n: first[n](k) + step * second[n](k) for n in range(SPACES)], table_jk, table_i)
     for slot in range(SLOTS):
         def edges(slot=slot):
             middle = [state_ref[slot, f] + step * rate_ref[slot, f] for f in range(FIELDS)]
@@ -489,7 +514,7 @@
     dev_count = lax.axis_size(axis)
     links = jnp.transpose(links, (0, 2, 1))
     counts = counts.reshape(1, 1)
-    send = pltpu.VMEM(SEND, f32)
+    sent = [pltpu.VMEM((2,) + SEND, f32), pltpu.VMEM((2,) + SEND, f32), pltpu.VMEM(SEND, f32)]
     block = pltpu.VMEM(state.shape, f32)
 
     def near_core(array):
@@ -499,27 +524,31 @@
 
     *sends, plan, limits = pl.pallas_call(
         lambda *refs: first_kernel(dev_count, axis, *refs),
-        out_shape=[send] * 4 + [jax.ShapeDtypeStruct((PLAN,), i32), pltpu.VMEM((dev_count, LANES), f32)],
+        out_shape=sent + [jax.ShapeDtypeStruct((PLAN,), i32), pltpu.VMEM((dev_count, LANES), f32)],
         in_specs=[in_smem()] * 3 + [in_vmem()],
-        out_specs=[in_vmem()] * 4 + [in_smem(), in_vmem()],
+        out_specs=[in_vmem()] * 3 + [in_smem(), in_vmem()],
         scratch_shapes=TABLES + (pltpu.SMEM((16,), i32),),
         name="faces",
     )(links, counts, block_metric, state)
 
+    def swapped(array, other):
+        return lax.ppermute(array, axis, [(p, other(p) % dev_count) for p in range(dev_count)])
+
     def exchanged(arrays):
-        result = []
-        for array, offset in zip(reversed(arrays), OFFSETS):
-            pairs = [((p + offset) % dev_count, p) for p in range(dev_count)]
-            result.append(lax.ppermute(array, axis, pairs))
-        return result
+        far = swapped(arrays[1], lambda p: p - 2 if p // 2 % 2 == 0 else p + 2)
+        near = swapped(arrays[0], lambda p: p + 2 if p // 2 % 2 == 0 else p - 2)
+        chip = swapped(arrays[2], lambda p: p ^ 1)
+        near_passed = swapped(near, lambda p: p ^ 1)
+        far_passed = swapped(far, lambda p: p ^ 1)
+        return [near, far, chip, near_passed, far_passed]
 
     limits = lax.all_to_all(limits, axis, 0, 0, tiled=True)
     first = exchanged(sends)
     rate, *sends_two = pl.pallas_call(
         second_kernel,
-        out_shape=[block] + [send] * 4,
-        in_specs=[in_smem()] * 5 + [in_vmem()] * 6,
-        out_specs=[in_vmem()] * 5,
+        out_shape=[block] + sent,
+        in_specs=[in_smem()] * 5 + [in_vmem()] * 7,
+        out_specs=[in_vmem()] * 4,
         scratch_shapes=SCRATCH,
         name="rate_one",
     )(links, counts, block_metric, inflow, plan, state_near, wall_dist, *map(near_core, first))
@@ -529,7 +558,7 @@
     tendency, step = pl.pallas_call(
         third_kernel,
         out_shape=[jax.ShapeDtypeStruct(state.shape, f32), jax.ShapeDtypeStruct((1, 1), f32)],
-        in_specs=[in_smem()] * 5 + [in_vmem()] * 12,
+        in_specs=[in_smem()] * 5 + [in_vmem()] * 14,
         out_specs=[in_vmem()] * 2,
         scratch_shapes=SCRATCH + (pltpu.VMEM(state.shape, f32),),
         name="rate_two",

time: 49.1 us -> 45.5 us (0.927)
  starting transfers between devices: 34.8 us -> 30.1 us
  waiting for transfers between devices: 3.49 us -> 4.45 us
    all_to_all x1, starting transfers between devices: 15.7 us -> 6.37 us  [body(): limits = lax.all_to_all(limits, axis, 0, 0, tiled=True)]
    ppermute x8 -> x10, starting transfers between devices: 19.1 us -> 23.8 us  [swapped(): lax.ppermute(array, axis, [(p, other(p) % dev_count) for p in range(dev_c...]
    ppermute x8 -> x10, waiting for transfers between devices: 3.49 us -> 4.45 us  [swapped(): lax.ppermute(array, axis, [(p, other(p) % dev_count) for p in range(dev_c...]
  transfers between devices with their start and end apart: 9 -> 11, of which waited for: 2 -> 3; matrix products, arithmetic and copies ran while one was open for 0% -> 0% of each run, Pallas kernels for 7% -> 7%
where the time goes in v2:
time: 45.5 us; the launch traced here: 45.2 us
  starting transfers between devices  30.1 us (66%)
  Pallas kernels  9.2 us (20%)
  waiting for transfers between devices  4.45 us (10%)
  between operations  1.39 us (3%)
    ppermute x10, starting transfers between devices, swapped(): lax.ppermute(array, axis, [(p, other(p) % dev_count) for p in range(dev_c...  23.8 us
    all_to_all x1, starting transfers between devices, body(): limits = lax.all_to_all(limits, axis, 0, 0, tiled=True)  6.37 us
    ppermute x10, waiting for transfers between devices, swapped(): lax.ppermute(array, axis, [(p, other(p) % dev_count) for p in range(dev_c...  4.45 us
    pallas_call x1, Pallas kernels, body(): pl.pallas_call(third_kernel, out_shape=[jax.ShapeDtypeStruct(state.shape,...  3.75 us
    pallas_call x1, Pallas kernels, body(): pl.pallas_call(second_kernel, out_shape=[block] + sent, in_specs=[in_smem...  3.23 us
    pallas_call x1, Pallas kernels, body(): pl.pallas_call(lambda *refs: first_kernel(dev_count, axis, *refs), out_sh...  2.23 us
  transfers between devices with their start and end apart: 11, of which 3 were waited for; matrix products, arithmetic and copies ran while one was open for 0% of the time, Pallas kernels for 7%

profile of v2, /device:TPU:1, one launch (start us, length us, event | category | flops | bytes accessed | tf_op | source)
XLA Modules:
  0.0 45.2 jit_solution(16209520917762875854)
XLA Ops:
  0.6 0.0 copy-start
  1.3 2.2 %faces.1 = (f32[2,8,8,128]{3,2,1,0:T(8,128)S(1)}, f32[2,8,8,128]{3,2,1,0:T(8,128)S(1)}, f32[8,8,128]{2,1,0:T(8,128)S(1)}, s32[128]{0:T(128)}, f32[256,128]{1,0:T(8,128)}) custom-call(s32[3,4,6]{2,1,0:T(4,128)} %bitcast.11, s32[1,1]{1,0:T(1,128)} %bitcast.7.refs_1_, f32[3,10]{1,0:T(4,128)} %metric_ref.3, f32[3,6,16,256]{3,2,1,0:T(8,128)} %state_ref.3), custom_call_target="tpu_custom_call" | custom-call | tf_op jit(solution)/shard_map/faces/pallas_call | solution.py:525
  3.6 2.1 %collective-permute-start = (f32[2,8,8,128]{3,2,1,0:T(8,128)S(1)}, f32[2,8,8,128]{3,2,1,0:T(8,128)S(1)}, u32[]{:S(2)}, u32[]{:S(2)}) collective-permute-start(f32[2,8,8,128]{3,2,1,0:T(8,128)S(1)} %get-tuple-element.14), channel_id=1, source_target_pairs={{0,2},{1,3},{2,0},{3,1},{4,6},{5,7},{6,4},{7,5},{8,10},{9,11},{10,... | collective-permute-start | bytes 196616 | tf_op jit(solution)/shard_map/ppermute | solution.py:535
  5.7 9.6 %collective-permute-start.1 = (f32[2,8,8,128]{3,2,1,0:T(8,128)S(1)}, f32[2,8,8,128]{3,2,1,0:T(8,128)S(1)}, u32[]{:S(2)}, u32[]{:S(2)}) collective-permute-start(f32[2,8,8,128]{3,2,1,0:T(8,128)S(1)} %get-tuple-element.15), channel_id=1, source_target_pairs={{0,254},{1,255},{2,4},{3,5},{4,2},{5,3},{6,8},{7,9},{8,6},{9,7},{1... | collective-permute-start | bytes 196616 | tf_op jit(solution)/shard_map/ppermute | solution.py:535
  15.2 0.0 copy-start.1
  15.2 6.4 %all-to-all-start = ((f32[256,1,128]{2,1,0:T(1,128)}), f32[256,1,128]{2,1,0:T(1,128)S(1)}, u32[]{:S(2)}, u32[]{:S(2)}) async-start(f32[256,1,128]{2,1,0:T(1,128)} %bitcast.3), calls=%async_computation | async-start | bytes 262144 | tf_op jit(solution)/shard_map/all_to_all | solution.py:545
  21.6 0.0 collective-permute-done.refs_0_
  21.6 2.4 %collective-permute-start.3 = (f32[2,8,8,128]{3,2,1,0:T(8,128)S(1)}, f32[2,8,8,128]{3,2,1,0:T(8,128)S(1)}, u32[]{:S(2)}, u32[]{:S(2)}) collective-permute-start(f32[2,8,8,128]{3,2,1,0:T(8,128)S(1)} %collective-permute-done.refs_0_), channel_id=1, source_target_pairs={{0,1},{1,0},{2,3},{3,2},{4,5},{5,4},{6,7},{7,6},{8,9},{9,8},{10,11... | collective-permute-start | bytes 196616 | tf_op jit(solution)/shard_map/ppermute | solution.py:535
  24.0 0.0 collective-permute-done.1.refs_1_
  24.0 0.1 collective-permute-start.4
  24.1 0.4 collective-permute-start.2
  24.5 0.9 %collective-permute-done.2.refs_2_ = f32[8,8,128]{2,1,0:T(8,128)S(1)} collective-permute-done((f32[8,8,128]{2,1,0:T(8,128)S(1)}, f32[8,8,128]{2,1,0:T(8,128)S(1)}, u32[]{:S(2)}, u32[]{:S(2)}) %collective-permute-start.2) | collective-permute-done | bytes 32800 | tf_op jit(solution)/shard_map/ppermute | solution.py:535
  25.4 0.0 collective-permute-done.3.refs_3_
  25.4 0.0 collective-permute-done.4.refs_4_
  25.4 0.0 copy-done
  25.4 0.0 copy-done.1
  25.4 3.2 %rate_one.1 = (f32[3,6,16,256]{3,2,1,0:T(8,128)S(1)}, f32[2,8,8,128]{3,2,1,0:T(8,128)S(1)}, f32[2,8,8,128]{3,2,1,0:T(8,128)S(1)}, f32[8,8,128]{2,1,0:T(8,128)S(1)}) custom-call(s32[3,4,6]{2,1,0:T(4,128)} %bitcast.12, s32[1,1]{1,0:T(1,128)} %bitcast.8.counts_ref, f32[3,10]{1,0:T(4,128)} %metric_ref.3, f32[6]{0:T(128)} %inflow_ref.3, ...), custom_call_target="tpu_custom_call" | custom-call | tf_op jit(solution)/shard_map/rate_one/pallas_call | solution.py:547
  28.6 0.1 collective-permute-start.5
  28.7 8.4 %collective-permute-start.6 = (f32[2,8,8,128]{3,2,1,0:T(8,128)S(1)}, f32[2,8,8,128]{3,2,1,0:T(8,128)S(1)}, u32[]{:S(2)}, u32[]{:S(2)}) collective-permute-start(f32[2,8,8,128]{3,2,1,0:T(8,128)S(1)} %get-tuple-element.19), channel_id=1, source_target_pairs={{0,254},{1,255},{2,4},{3,5},{4,2},{5,3},{6,8},{7,9},{8,6},{9,7},{1... | collective-permute-start | bytes 196616 | tf_op jit(solution)/shard_map/ppermute | solution.py:535
  37.2 0.0 collective-permute-done.5.refs_5_
  37.2 0.2 collective-permute-start.8
  37.3 2.4 %collective-permute-done.6.refs_6_ = f32[2,8,8,128]{3,2,1,0:T(8,128)S(1)} collective-permute-done((f32[2,8,8,128]{3,2,1,0:T(8,128)S(1)}, f32[2,8,8,128]{3,2,1,0:T(8,128)S(1)}, u32[]{:S(2)}, u32[]{:S(2)}) %collective-permute-start.6) | collective-permute-done | bytes 65568 | tf_op jit(solution)/shard_map/ppermute | solution.py:535
  39.8 0.5 %collective-permute-start.9 = (f32[2,8,8,128]{3,2,1,0:T(8,128)S(1)}, f32[2,8,8,128]{3,2,1,0:T(8,128)S(1)}, u32[]{:S(2)}, u32[]{:S(2)}) collective-permute-start(f32[2,8,8,128]{3,2,1,0:T(8,128)S(1)} %collective-permute-done.6.refs_6_), channel_id=1, source_target_pairs={{0,1},{1,0},{2,3},{3,2},{4,5},{5,4},{6,7},{7,6},{8,9},{9,8},{10,11... | collective-permute-start | bytes 196616 | tf_op jit(solution)/shard_map/ppermute | solution.py:535
  40.2 0.0 collective-permute-start.7
  40.3 1.2 %collective-permute-done.7.refs_7_ = f32[8,8,128]{2,1,0:T(8,128)S(1)} collective-permute-done((f32[8,8,128]{2,1,0:T(8,128)S(1)}, f32[8,8,128]{2,1,0:T(8,128)S(1)}, u32[]{:S(2)}, u32[]{:S(2)}) %collective-permute-start.7) | collective-permute-done | bytes 32800 | tf_op jit(solution)/shard_map/ppermute | solution.py:535
  41.4 0.0 all-to-all-done
  41.4 0.0 collective-permute-done.8.refs_8_
  41.4 0.0 collective-permute-done.9.refs_9_
  41.4 3.8 %rate_two.1 = (f32[3,6,16,256]{3,2,1,0:T(8,128)}, f32[1,1]{1,0:T(1,128)}) custom-call(s32[3,4,6]{2,1,0:T(4,128)} %bitcast.13, s32[1,1]{1,0:T(1,128)} %bitcast.9.counts_ref, f32[3,10]{1,0:T(4,128)} %metric_ref.3, f32[6]{0:T(128)} %inflow_ref.3, s32[128]{0:T(128)} %get-tuple-element.13.plan_ref, f32[3,6,16,256]{3,2,1,0:T(8,128)S(1)} %copy-done, ...), custom_call_target="tpu_custom_call" | custom-call | tf_op jit(solution)/shard_map/rate_two/pallas_call | solution.py:558
Async XLA Ops:
  0.6 24.8 %copy-start = (f32[3,6,16,256]{3,2,1,0:T(8,128)S(1)}, f32[3,6,16,256]{3,2,1,0:T(8,128)}, u32[]{:S(2)}) copy-start(f32[3,6,16,256]{3,2,1,0:T(8,128)} %state_ref.3) | copy-start | bytes 884740
  3.6 18.1 %collective-permute-start = (f32[2,8,8,128]{3,2,1,0:T(8,128)S(1)}, f32[2,8,8,128]{3,2,1,0:T(8,128)S(1)}, u32[]{:S(2)}, u32[]{:S(2)}) collective-permute-start(f32[2,8,8,128]{3,2,1,0:T(8,128)S(1)} %get-tuple-element.14), channel_id=1, source_target_pairs={{0,2},{1,3},{2,0},{3,1},{4,6},{5,7},{6,4},{7,5},{8,10},{9,11},{10,... | collective-permute-start | bytes 196616 | tf_op jit(solution)/shard_map/ppermute | solution.py:535
  5.7 18.3 %collective-permute-start.1 = (f32[2,8,8,128]{3,2,1,0:T(8,128)S(1)}, f32[2,8,8,128]{3,2,1,0:T(8,128)S(1)}, u32[]{:S(2)}, u32[]{:S(2)}) collective-permute-start(f32[2,8,8,128]{3,2,1,0:T(8,128)S(1)} %get-tuple-element.15), channel_id=1, source_target_pairs={{0,254},{1,255},{2,4},{3,5},{4,2},{5,3},{6,8},{7,9},{8,6},{9,7},{1... | collective-permute-start | bytes 196616 | tf_op jit(solution)/shard_map/ppermute | solution.py:535
  15.2 10.2 %copy-start.1 = (f32[3,16,256]{2,1,0:T(8,128)S(1)}, f32[3,16,256]{2,1,0:T(8,128)}, u32[]{:S(2)}) copy-start(f32[3,16,256]{2,1,0:T(8,128)} %distance_ref.3) | copy-start | bytes 147460
  15.2 26.2 %all-to-all-start = ((f32[256,1,128]{2,1,0:T(1,128)}), f32[256,1,128]{2,1,0:T(1,128)S(1)}, u32[]{:S(2)}, u32[]{:S(2)}) async-start(f32[256,1,128]{2,1,0:T(1,128)} %bitcast.3), calls=%async_computation | async-start | bytes 262144 | tf_op jit(solution)/shard_map/all_to_all | solution.py:545
  21.6 3.7 %collective-permute-start.3 = (f32[2,8,8,128]{3,2,1,0:T(8,128)S(1)}, f32[2,8,8,128]{3,2,1,0:T(8,128)S(1)}, u32[]{:S(2)}, u32[]{:S(2)}) collective-permute-start(f32[2,8,8,128]{3,2,1,0:T(8,128)S(1)} %collective-permute-done.refs_0_), channel_id=1, source_target_pairs={{0,1},{1,0},{2,3},{3,2},{4,5},{5,4},{6,7},{7,6},{8,9},{9,8},{10,11... | collective-permute-start | bytes 196616 | tf_op jit(solution)/shard_map/ppermute | solution.py:535
  24.0 1.4 %collective-permute-start.4 = (f32[2,8,8,128]{3,2,1,0:T(8,128)S(1)}, f32[2,8,8,128]{3,2,1,0:T(8,128)S(1)}, u32[]{:S(2)}, u32[]{:S(2)}) collective-permute-start(f32[2,8,8,128]{3,2,1,0:T(8,128)S(1)} %collective-permute-done.1.refs_1_), channel_id=1, source_target_pairs={{0,1},{1,0},{2,3},{3,2},{4,5},{5,4},{6,7},{7,6},{8,9},{9,8},{10,11... | collective-permute-start | bytes 196616 | tf_op jit(solution)/shard_map/ppermute | solution.py:535
  24.1 1.3 %collective-permute-start.2 = (f32[8,8,128]{2,1,0:T(8,128)S(1)}, f32[8,8,128]{2,1,0:T(8,128)S(1)}, u32[]{:S(2)}, u32[]{:S(2)}) collective-permute-start(f32[8,8,128]{2,1,0:T(8,128)S(1)} %get-tuple-element.16), channel_id=1, source_target_pairs={{0,1},{1,0},{2,3},{3,2},{4,5},{5,4},{6,7},{7,6},{8,9},{9,8},{10,11... | collective-permute-start | bytes 98312 | tf_op jit(solution)/shard_map/ppermute | solution.py:535
  28.6 8.5 %collective-permute-start.5 = (f32[2,8,8,128]{3,2,1,0:T(8,128)S(1)}, f32[2,8,8,128]{3,2,1,0:T(8,128)S(1)}, u32[]{:S(2)}, u32[]{:S(2)}) collective-permute-start(f32[2,8,8,128]{3,2,1,0:T(8,128)S(1)} %get-tuple-element.18), channel_id=1, source_target_pairs={{0,2},{1,3},{2,0},{3,1},{4,6},{5,7},{6,4},{7,5},{8,10},{9,11},{10,... | collective-permute-start | bytes 196616 | tf_op jit(solution)/shard_map/ppermute | solution.py:535
  28.7 11.0 %collective-permute-start.6 = (f32[2,8,8,128]{3,2,1,0:T(8,128)S(1)}, f32[2,8,8,128]{3,2,1,0:T(8,128)S(1)}, u32[]{:S(2)}, u32[]{:S(2)}) collective-permute-start(f32[2,8,8,128]{3,2,1,0:T(8,128)S(1)} %get-tuple-element.19), channel_id=1, source_target_pairs={{0,254},{1,255},{2,4},{3,5},{4,2},{5,3},{6,8},{7,9},{8,6},{9,7},{1... | collective-permute-start | bytes 196616 | tf_op jit(solution)/shard_map/ppermute | solution.py:535
  37.2 4.3 %collective-permute-start.8 = (f32[2,8,8,128]{3,2,1,0:T(8,128)S(1)}, f32[2,8,8,128]{3,2,1,0:T(8,128)S(1)}, u32[]{:S(2)}, u32[]{:S(2)}) collective-permute-start(f32[2,8,8,128]{3,2,1,0:T(8,128)S(1)} %collective-permute-done.5.refs_5_), channel_id=1, source_target_pairs={{0,1},{1,0},{2,3},{3,2},{4,5},{5,4},{6,7},{7,6},{8,9},{9,8},{10,11... | collective-permute-start | bytes 196616 | tf_op jit(solution)/shard_map/ppermute | solution.py:535
  39.8 1.7 %collective-permute-start.9 = (f32[2,8,8,128]{3,2,1,0:T(8,128)S(1)}, f32[2,8,8,128]{3,2,1,0:T(8,128)S(1)}, u32[]{:S(2)}, u32[]{:S(2)}) collective-permute-start(f32[2,8,8,128]{3,2,1,0:T(8,128)S(1)} %collective-permute-done.6.refs_6_), channel_id=1, source_target_pairs={{0,1},{1,0},{2,3},{3,2},{4,5},{5,4},{6,7},{7,6},{8,9},{9,8},{10,11... | collective-permute-start | bytes 196616 | tf_op jit(solution)/shard_map/ppermute | solution.py:535
  40.2 1.2 %collective-permute-start.7 = (f32[8,8,128]{2,1,0:T(8,128)S(1)}, f32[8,8,128]{2,1,0:T(8,128)S(1)}, u32[]{:S(2)}, u32[]{:S(2)}) collective-permute-start(f32[8,8,128]{2,1,0:T(8,128)S(1)} %get-tuple-element.20), channel_id=1, source_target_pairs={{0,1},{1,0},{2,3},{3,2},{4,5},{5,4},{6,7},{7,6},{8,9},{9,8},{10,11... | collective-permute-start | bytes 98312 | tf_op jit(solution)/shard_map/ppermute | solution.py:535
